TPU v7x, 32 devices: a whole 2x2x4 slice. The times are simulated.
32 devices in a mesh: replica: 8 (over z, x), tensor: 4 (over y, core).
Axes of the slice: x: 2, y: 2, z: 4, core: 2. Of those that a mesh axis runs over, the one named last changes fastest.
Arguments:
- hidden_acts: bfloat16 [4096, 16384], P('replica', 'tensor'), may hold values from -6 to 6
- out_grad: bfloat16 [4096, 768], P('replica'), may hold values from -0.25 to 0.25
- error_prev: bfloat16 [8, 768, 16384], P('replica', None, 'tensor'), may hold values from -6 to 6
- right_prev: bfloat16 [16384, 128], P('tensor'), may hold values from -6 to 6
Outputs:
- error_next: bfloat16 [8, 768, 16384], P('replica', None, 'tensor')
- right_next: float32 [16384, 128], P('tensor')
All inputs are finite; a program needn't handle non-finite values.
Results may differ from a plain program's by a relative error of at most 0.0058.
Values may be sent and summed in bfloat16 or wider, within the bound.
A program may use at most 64 MiB of HBM per device.

v0:
```python
import jax
import jax.numpy as jnp
from jax import lax
from jax.sharding import PartitionSpec as P


def orthonormal(p_rows, gram_matrix):
    factor = jnp.linalg.cholesky(gram_matrix)
    return jax.scipy.linalg.solve_triangular(factor, p_rows.T, lower=True).T.astype(jnp.bfloat16)


def shards(hidden_acts, out_grad, error_prev, right_prev):
    weight_grad = lax.dot_general(
        out_grad, hidden_acts, (((0,), (0,)), ((), ())), preferred_element_type=jnp.float32
    )
    compensated = (weight_grad + error_prev[0].astype(jnp.float32)).astype(jnp.bfloat16)
    partial_value = jnp.dot(compensated, right_prev, preferred_element_type=jnp.float32)
    p_sum = lax.psum(partial_value, ("replica", "tensor"))
    gram_matrix = jnp.dot(p_sum.T, p_sum, precision=lax.Precision.HIGHEST)
    left_low = orthonormal(p_sum, gram_matrix)
    replicas = lax.axis_size("replica")
    right_terms = lax.dot_general(
        compensated, left_low, (((0,), (0,)), ((), ())), preferred_element_type=jnp.float32
    )
    right_next = lax.psum(right_terms, "replica") / replicas
    right_low = right_next.astype(jnp.bfloat16)
    approx = lax.dot_general(
        left_low, right_low, (((1,), (1,)), ((), ())), preferred_element_type=jnp.float32
    )
    error_next = (compensated.astype(jnp.float32) - approx).astype(jnp.bfloat16)
    return (error_next[None], right_next)


def solution(mesh):
    return jax.shard_map(
        shards,
        mesh=mesh,
        in_specs=(
            P("replica", "tensor"),
            P("replica", None),
            P("replica", None, "tensor"),
            P("tensor", None),
        ),
        out_specs=(P("replica", None, "tensor"), P("tensor", None)),
        check_vma=False,
    )
```

profile of v0, /device:TPU:0, one launch (start us, length us, event | category | flops | bytes accessed | tf_op | source)
XLA Modules:
  0.0 302.5 jit_solution(8270023553574536663)
XLA Ops:
  7.2 0.0 copy-start
  7.2 0.0 all-reduce.3.cloned.1.call-start
  7.2 7.8 %fusion = bf16[768,4096]{1,0:T(8,128)(2,1)S(1)} fusion(bf16[512,768]{1,0:T(8,128)(2,1)} %param.5, bf16[512,4096]{1,0:T(8,128)(2,1)} %param.4, bf16[1,768,4096]{2,1,0:T(8,128)(2,1)} %param.6), kind=kOutput, calls=%fused_computation.1 | convolution fusion | flops 3230662656 | bytes 17563648 | tf_op jit(solution)/shard_map/dot_general | solution.py:13
  15.1 0.0 copy-start.1
  15.1 2.7 copy-done.1
  17.8 0.0 copy-done
  17.8 2.5 fusion.6
  20.3 0.0 all-reduce.3.cloned.1.call-update
  20.3 0.2 all-reduce.5.cloned.1.call-start
  20.6 131.4 %all-reduce.3.cloned.1.call-done = f32[768,128]{1,0:T(8,128)} async-done(((f32[768,128]{1,0:T(8,128)}), f32[768,128]{1,0:T(8,128)}) %all-reduce.3.cloned.1.call-update) | async-done | bytes 393232 | tf_op jit(solution)/shard_map/psum | solution.py:18
  152.0 1.9 fusion.7
  153.9 0.1 copy.6
  154.0 11.7 %cholesky.16 = f32[128,128]{1,0:T(8,128)S(1)} custom-call(f32[128,128]{1,0:T(8,128)S(1)} %fusion.5), custom_call_target="Cholesky" | custom-call | tf_op jit(solution)/shard_map/jit(cholesky)/cholesky | solution.py:8
  165.8 0.6 compare_reduce_fusion
  166.4 0.7 fusion.3
  167.1 9.8 %custom-call.7 = f32[1,128,128]{1,2,0:T(8,128)S(1)} custom-call(f32[1,128,128]{2,1,0:T(8,128)S(1)} %fusion.3), custom_call_target="InvertDiagBlocksLowerTriangular" | custom-call | tf_op jit(solution)/shard_map/jit(_solve_triangular)/triangular_solve | solution.py:9
  176.9 1.5 convolution_convert_fusion
  178.3 5.9 %fusion.8 = f32[4096,128]{1,0:T(8,128)} fusion(bf16[768,4096]{1,0:T(8,128)(2,1)} %copy-done.1, bf16[768,128]{1,0:T(8,128)(2,1)S(1)} %convolution_convert_fusion), kind=kOutput, calls=%fused_computation.18 | convolution fusion | flops 805306368 | bytes 8585216 | tf_op jit(solution)/shard_map/dot_general | solution.py:22
  184.3 0.0 all-reduce.5.cloned.1.call-update
  184.3 101.5 %all-reduce.5.cloned.1.call-done = f32[4096,128]{1,0:T(8,128)} async-done(((f32[4096,128]{1,0:T(8,128)}), f32[4096,128]{1,0:T(8,128)}) %all-reduce.5.cloned.1.call-update) | async-done | bytes 2097168 | tf_op jit(solution)/shard_map/psum | solution.py:25
  285.8 1.7 broadcast_multiply_fusion
  287.5 0.0 copy-start.2
  287.6 8.1 %fusion.1 = bf16[1,768,4096]{2,1,0:T(8,128)(2,1)} fusion(bf16[768,128]{1,0:T(8,128)(2,1)S(1)} %convolution_convert_fusion, bf16[768,4096]{1,0:T(8,128)(2,1)} %copy-done.1, f32[4096,128]{1,0:T(8,128)S(1)} %broadcast_multiply_fusion), kind=kOutput, calls=%fused_computation.3 | convolution fusion | flops 815267840 | bytes 14876672 | tf_op jit(solution)/shard_map/dot_general | solution.py:27
  295.6 0.0 copy-done.2
  (2 shorter events, 0.0 us)
Async XLA Ops:
  7.2 10.6 %copy-start = (bf16[4096,128]{1,0:T(8,128)(2,1)S(1)}, bf16[4096,128]{1,0:T(8,128)(2,1)}, u32[]{:S(2)}) copy-start(bf16[4096,128]{1,0:T(8,128)(2,1)} %param.7) | copy-start | bytes 3145732
  7.2 144.8 %all-reduce.3.cloned.1.call-start = ((), (), s32[]{:S(2)}) async-start(), calls=%async_computation | async-start | bytes 786432 | tf_op jit(solution)/shard_map/psum | solution.py:18
  15.1 2.7 copy-start.1
  20.3 265.5 %all-reduce.5.cloned.1.call-start = ((), (), s32[]{:S(2)}) async-start(), calls=%async_computation.1 | async-start | bytes 4194304 | tf_op jit(solution)/shard_map/psum | solution.py:25
  287.5 8.1 %copy-start.2 = (f32[4096,128]{1,0:T(8,128)}, f32[4096,128]{1,0:T(8,128)S(1)}, u32[]{:S(2)}) copy-start(f32[4096,128]{1,0:T(8,128)S(1)} %broadcast_multiply_fusion) | copy-start | bytes 6291460
Sparse Core Ops, SparseCore 0:
  20.5 131.4 all-reduce.2
  184.4 101.3 all-reduce.4
where the time goes:
time: 303 us; the launch traced here: 302 us
  waiting for transfers between devices  233 us (77%)
  matrix products  27.7 us (9%)
  other arithmetic  24.6 us (8%)
  between operations  14.1 us (5%)
    psum x1, waiting for transfers between devices, shards(): p_sum = lax.psum(partial_value, ('replica', 'tensor'))  131 us
    psum x1, waiting for transfers between devices, shards(): right_next = lax.psum(right_terms, 'replica') / replicas  102 us
    another operation x3, other arithmetic, orthonormal(): factor = jnp.linalg.cholesky(gram_matrix)  12.4 us
    another operation x2, other arithmetic, orthonormal(): jax.scipy.linalg.solve_triangular(factor, p_rows.T, lower=True)  10.5 us
    dot_general x1, matrix products, shards(): lax.dot_general(left_low, right_low, (((1,), (1,)), ((), ())), preferred_...  8.05 us
    dot_general x1, matrix products, shards(): lax.dot_general(out_grad, hidden_acts, (((0,), (0,)), ((), ())), preferre...  7.83 us
  transfers between devices with their start and end apart: 2, of which 2 were waited for; matrix products, arithmetic and copies ran while one was open for 0% of the time, Pallas kernels for 0%

commit v1 on v0

--- a/solution.py
+++ b/solution.py
@@ -1,7 +1,175 @@
+import functools
+
 import jax
 import jax.numpy as jnp
 from jax import lax
+from jax.experimental import pallas as pl
+from jax.experimental.pallas import tpu as pltpu
 from jax.sharding import PartitionSpec as P
+
+MESH = pl.DeviceIdType.MESH
+VMEM = pl.BlockSpec(memory_space=pltpu.VMEM)
+
+
+def wait_bytes(view, sem):
+    pltpu.make_async_copy(view, view, sem).wait()
+
+
+def left_kernel(replicas, tensors, piece, x_ref, out_ref, recv, mine, gathered, send_sem, recv_sem, send2_sem, recv2_sem):
+    count = replicas * tensors
+    me = lax.axis_index("replica") * tensors + lax.axis_index("tensor")
+
+    def peer(k):
+        other = lax.rem(me + k, count)
+        return other, (other // tensors, lax.rem(other, tensors))
+
+    barrier = pltpu.get_barrier_semaphore()
+
+    def greet(k, carry):
+        pl.semaphore_signal(barrier, inc=1, device_id=peer(k)[1], device_id_type=MESH)
+        return carry
+
+    lax.fori_loop(1, count, greet, 0)
+    pl.semaphore_wait(barrier, count - 1)
+
+    def scatter(k, carry):
+        other, where = peer(k)
+        pltpu.make_async_remote_copy(
+            src_ref=x_ref.at[other], dst_ref=recv.at[k - 1], send_sem=send_sem, recv_sem=recv_sem,
+            device_id=where, device_id_type=MESH,
+        ).start()
+        return carry
+
+    lax.fori_loop(1, count, scatter, 0)
+    wait_bytes(recv, recv_sem)
+    mine[...] = x_ref[me] + jnp.sum(recv[...], axis=0)
+
+    def gather(k, carry):
+        other, where = peer(k)
+        pltpu.make_async_remote_copy(
+            src_ref=mine, dst_ref=gathered.at[me], send_sem=send2_sem, recv_sem=recv2_sem,
+            device_id=where, device_id_type=MESH,
+        ).start()
+        return carry
+
+    lax.fori_loop(1, count, gather, 0)
+    gathered[me] = mine[...]
+    wait_bytes(recv, recv2_sem)
+    out_ref[...] = gathered[...]
+    wait_bytes(recv, send_sem)
+    wait_bytes(recv, send2_sem)
+
+
+def left_sum(partial_value, replicas, tensors):
+    rows, rank = partial_value.shape
+    count = replicas * tensors
+    piece = -(-rows // (count * 8)) * 8
+    padded = jnp.pad(partial_value, ((0, count * piece - rows), (0, 0))).reshape(count, piece, rank)
+    out = pl.pallas_call(
+        functools.partial(left_kernel, replicas, tensors, piece),
+        out_shape=jax.ShapeDtypeStruct((count, piece, rank), jnp.float32),
+        in_specs=[VMEM],
+        out_specs=VMEM,
+        scratch_shapes=[
+            pltpu.VMEM((count - 1, piece, rank), jnp.float32),
+            pltpu.VMEM((piece, rank), jnp.float32),
+            pltpu.VMEM((count, piece, rank), jnp.float32),
+            pltpu.SemaphoreType.DMA, pltpu.SemaphoreType.DMA, pltpu.SemaphoreType.DMA, pltpu.SemaphoreType.DMA,
+        ],
+        compiler_params=pltpu.CompilerParams(collective_id=0, has_side_effects=True),
+    )(padded)
+    return out.reshape(count * piece, rank)[:rows]
+
+
+def right_kernel(replicas, inner, chunks, x_ref, out_ref, sendx, recvx, sendz, recvz, final, gathz, gathx,
+                 sx, rx, sz, rz, sg, rg, sh, rh):
+    outer = replicas // inner
+    me = lax.axis_index("replica")
+    mz, mx = me // inner, lax.rem(me, inner)
+    px = lax.rem(mx + 1, inner)
+    partner = {"replica": mz * inner + px}
+
+    def zpeer(k):
+        oz = lax.rem(mz + k, outer)
+        return oz, {"replica": oz * inner + mx}
+
+    barrier = pltpu.get_barrier_semaphore()
+    pl.semaphore_signal(barrier, inc=1, device_id=partner, device_id_type=MESH)
+    for k in range(1, outer):
+        pl.semaphore_signal(barrier, inc=1, device_id=zpeer(k)[1], device_id_type=MESH)
+    pl.semaphore_wait(barrier, outer)
+
+    for c in range(chunks):
+        sendx[c] = x_ref[px, :, c].astype(jnp.bfloat16)
+        if True:
+            pltpu.make_async_remote_copy(
+                src_ref=sendx.at[c], dst_ref=recvx.at[c], send_sem=sx.at[c], recv_sem=rx.at[c],
+                device_id=partner, device_id_type=MESH,
+            ).start()
+    for c in range(chunks):
+        wait_bytes(recvx.at[c], rx.at[c])
+        sendz[c] = (x_ref[mx, :, c] + recvx[c].astype(jnp.float32)).astype(jnp.bfloat16)
+        for k in range(1, outer):
+            oz, where = zpeer(k)
+            pltpu.make_async_remote_copy(
+                src_ref=sendz.at[c, oz], dst_ref=recvz.at[c, k - 1], send_sem=sz.at[c], recv_sem=rz.at[c],
+                device_id=where, device_id_type=MESH,
+            ).start()
+    for c in range(chunks):
+        wait_bytes(recvz.at[c], rz.at[c])
+        own = x_ref[mx, mz, c] + recvx[c, mz].astype(jnp.float32)
+        total = own + jnp.sum(recvz[c].astype(jnp.float32), axis=0)
+        final[c] = (total / replicas).astype(jnp.bfloat16)
+        for k in range(1, outer):
+            oz, where = zpeer(k)
+            pltpu.make_async_remote_copy(
+                src_ref=final.at[c], dst_ref=gathz.at[c, mz], send_sem=sg.at[c], recv_sem=rg.at[c],
+                device_id=where, device_id_type=MESH,
+            ).start()
+        gathz[c, mz] = final[c]
+    for c in range(chunks):
+        wait_bytes(recvz.at[c], rg.at[c])
+        pltpu.make_async_remote_copy(
+            src_ref=gathz.at[c], dst_ref=gathx.at[c], send_sem=sh.at[c], recv_sem=rh.at[c],
+            device_id=partner, device_id_type=MESH,
+        ).start()
+        out_ref[mx, :, c] = gathz[c]
+    for c in range(chunks):
+        wait_bytes(gathx.at[c], rh.at[c])
+        out_ref[px, :, c] = gathx[c]
+    for c in range(chunks):
+        wait_bytes(sendx.at[c], sx.at[c])
+        wait_bytes(recvz.at[c], sz.at[c])
+        wait_bytes(recvz.at[c], sg.at[c])
+        wait_bytes(gathz.at[c], sh.at[c])
+
+
+def right_mean(terms, replicas):
+    width, rank = terms.shape
+    inner = 2
+    outer = replicas // inner
+    rows = width // replicas
+    chunks = next(c for c in (4, 2, 1) if rows % (c * 16) == 0)
+    rows //= chunks
+    shape = (inner, outer, chunks, rows, rank)
+    bf = jnp.bfloat16
+    out = pl.pallas_call(
+        functools.partial(right_kernel, replicas, inner, chunks),
+        out_shape=jax.ShapeDtypeStruct(shape, bf),
+        in_specs=[VMEM],
+        out_specs=VMEM,
+        scratch_shapes=[
+            pltpu.VMEM((chunks, outer, rows, rank), bf),
+            pltpu.VMEM((chunks, outer, rows, rank), bf),
+            pltpu.VMEM((chunks, outer, rows, rank), bf),
+            pltpu.VMEM((chunks, outer - 1, rows, rank), bf),
+            pltpu.VMEM((chunks, rows, rank), bf),
+            pltpu.VMEM((chunks, outer, rows, rank), bf),
+            pltpu.VMEM((chunks, outer, rows, rank), bf),
+        ] + [pltpu.SemaphoreType.DMA((chunks,))] * 8,
+        compiler_params=pltpu.CompilerParams(collective_id=1, has_side_effects=True),
+    )(terms.reshape(shape))
+    return out.reshape(width, rank)
 
 
 def orthonormal(p_rows, gram_matrix):
@@ -10,20 +178,20 @@
 
 
 def shards(hidden_acts, out_grad, error_prev, right_prev):
+    replicas, tensors = lax.axis_size("replica"), lax.axis_size("tensor")
     weight_grad = lax.dot_general(
         out_grad, hidden_acts, (((0,), (0,)), ((), ())), preferred_element_type=jnp.float32
     )
     compensated = (weight_grad + error_prev[0].astype(jnp.float32)).astype(jnp.bfloat16)
     partial_value = jnp.dot(compensated, right_prev, preferred_element_type=jnp.float32)
-    p_sum = lax.psum(partial_value, ("replica", "tensor"))
+    p_sum = left_sum(partial_value, replicas, tensors)
     gram_matrix = jnp.dot(p_sum.T, p_sum, precision=lax.Precision.HIGHEST)
     left_low = orthonormal(p_sum, gram_matrix)
-    replicas = lax.axis_size("replica")
     right_terms = lax.dot_general(
         compensated, left_low, (((0,), (0,)), ((), ())), preferred_element_type=jnp.float32
     )
-    right_next = lax.psum(right_terms, "replica") / replicas
-    right_low = right_next.astype(jnp.bfloat16)
+    right_low = right_mean(right_terms, replicas)
+    right_next = right_low.astype(jnp.float32)
     approx = lax.dot_general(
         left_low, right_low, (((1,), (1,)), ((), ())), preferred_element_type=jnp.float32
     )

time: 303 us -> 125 us (0.41)
  waiting for transfers between devices: 233 us -> 0 us
  Pallas kernels: 0 us -> 69.3 us
  between operations: 14.1 us -> 0.73 us
    psum x2 -> x0, waiting for transfers between devices: 233 us -> none  [the longest x1 131 us: shards(): p_sum = lax.psum(partial_value, ('replica', 'tensor'))]
    pallas_call x0 -> x2, Pallas kernels: none -> 69.3 us  [the longest x1 44.5 us: right_mean(): pl.pallas_call(functools.partial(right_kernel, replicas, inner, chunks),...]
  transfers between devices with their start and end apart: 2 -> 0, of which waited for: 2 -> 0; matrix products, arithmetic and copies ran while one was open for 0% -> 0% of each run, Pallas kernels for 0% -> 0%
where the time goes in v1:
time: 125 us
  Pallas kernels  69.3 us (55%)
  matrix products  27.4 us (22%)
  other arithmetic  24.4 us (20%)
  local copies, waits for them, and re-layouts  2.8 us (2%)
    pallas_call x1, Pallas kernels, right_mean(): pl.pallas_call(functools.partial(right_kernel, replicas, inner, chunks),...  44.5 us
    pallas_call x1, Pallas kernels, left_sum(): pl.pallas_call(functools.partial(left_kernel, replicas, tensors, piece),...  24.8 us
    another operation x3, other arithmetic, orthonormal(): factor = jnp.linalg.cholesky(gram_matrix)  12.4 us
    another operation x2, other arithmetic, orthonormal(): jax.scipy.linalg.solve_triangular(factor, p_rows.T, lower=True)  10.5 us
    dot_general x1, matrix products, shards(): lax.dot_general(out_grad, hidden_acts, (((0,), (0,)), ((), ())), preferre...  7.85 us
    dot_general x1, matrix products, shards(): lax.dot_general(left_low, right_low, (((1,), (1,)), ((), ())), preferred_...  7.7 us
    dot_general x1, matrix products, shards(): lax.dot_general(compensated, left_low, (((0,), (0,)), ((), ())), preferre...  5.94 us
    unnamed x6, local copies, waits for them, and re-layouts  2.71 us

profile of v1, /device:TPU:0, one launch (start us, length us, event | category | flops | bytes accessed | tf_op | source)
XLA Modules:
  0.0 124.6 jit_solution(15480653385987353994)
XLA Ops:
  0.6 0.0 copy-start
  0.6 7.8 %fusion = bf16[768,4096]{1,0:T(8,128)(2,1)S(1)} fusion(bf16[512,768]{1,0:T(8,128)(2,1)} %param.5, bf16[512,4096]{1,0:T(8,128)(2,1)} %param.4, bf16[1,768,4096]{2,1,0:T(8,128)(2,1)} %param.6), kind=kOutput, calls=%fused_computation.1 | convolution fusion | flops 3230662656 | bytes 17563648 | tf_op jit(solution)/shard_map/dot_general | solution.py:182
  8.5 0.0 copy-start.1
  8.5 2.7 %copy-done.1 = bf16[768,4096]{1,0:T(8,128)(2,1)} copy-done((bf16[768,4096]{1,0:T(8,128)(2,1)}, bf16[768,4096]{1,0:T(8,128)(2,1)S(1)}, u32[]{:S(2)}) %copy-start.1) | copy-done | bytes 6291480
  11.2 0.0 copy-done
  11.2 2.5 %fusion.5 = f32[768,128]{1,0:T(8,128)} fusion(bf16[768,4096]{1,0:T(8,128)(2,1)S(1)} %fusion, bf16[4096,128]{1,0:T(8,128)(2,1)S(1)} %copy-done), kind=kOutput, calls=%fused_computation.16 | convolution fusion | flops 805306368 | bytes 7733248 | tf_op jit(solution)/shard_map/dot_general | solution.py:186
  13.7 24.8 %shard_map.59 = f32[32,24,128]{2,1,0:T(8,128)} custom-call(f32[32,24,128]{2,1,0:T(8,128)} %bitcast.35), custom_call_target="tpu_custom_call" | custom-call | tf_op jit(solution)/shard_map/pallas_call | solution.py:68
  38.6 1.9 %convolution_bitcast_fusion = f32[128,128]{1,0:T(8,128)S(1)} fusion(f32[32,24,128]{2,1,0:T(8,128)} %shard_map.59), kind=kOutput, calls=%fused_computation.5 | convolution fusion | flops 150994944 | bytes 458752 | tf_op jit(solution)/shard_map/dot_general | solution.py:188
  40.5 0.1 copy.8
  40.6 11.7 %cholesky.16 = f32[128,128]{1,0:T(8,128)S(1)} custom-call(f32[128,128]{1,0:T(8,128)S(1)} %fusion.4), custom_call_target="Cholesky" | custom-call | tf_op jit(solution)/shard_map/jit(cholesky)/cholesky | solution.py:176
  52.3 0.6 compare_reduce_fusion
  53.0 0.7 fusion.2
  53.6 9.8 %custom-call.7 = f32[1,128,128]{1,2,0:T(8,128)S(1)} custom-call(f32[1,128,128]{2,1,0:T(8,128)S(1)} %fusion.2), custom_call_target="InvertDiagBlocksLowerTriangular" | custom-call | tf_op jit(solution)/shard_map/jit(_solve_triangular)/triangular_solve | solution.py:177
  63.5 1.5 %convolution_convert_fusion = bf16[768,128]{1,0:T(8,128)(2,1)S(1)} fusion(f32[768,128]{1,0:T(8,128)} %bitcast.34, f32[1,128,128]{1,2,0:T(8,128)S(1)} %custom-call.7), kind=kOutput, calls=%fused_computation.4 | convolution fusion | flops 151093248 | bytes 655360 | tf_op jit(solution)/shard_map/jit(_solve_triangular)/triangular_solve | solution.py:177
  64.9 5.9 %fusion.6 = f32[4096,128]{1,0:T(8,128)} fusion(bf16[768,4096]{1,0:T(8,128)(2,1)} %copy-done.1, bf16[768,128]{1,0:T(8,128)(2,1)S(1)} %convolution_convert_fusion), kind=kOutput, calls=%fused_computation.17 | convolution fusion | flops 805306368 | bytes 8585216 | tf_op jit(solution)/shard_map/dot_general | solution.py:190
  70.9 44.5 %shard_map.60 = bf16[2,4,4,128,128]{4,3,2,1,0:T(8,128)(2,1)} custom-call(f32[2,4,4,128,128]{4,3,2,1,0:T(8,128)} %bitcast.32), custom_call_target="tpu_custom_call" | custom-call | tf_op jit(solution)/shard_map/pallas_call | solution.py:156
  115.4 0.0 copy-start.2
  115.4 7.7 %fusion.1 = bf16[1,768,4096]{2,1,0:T(8,128)(2,1)} fusion(bf16[768,128]{1,0:T(8,128)(2,1)S(1)} %convolution_convert_fusion, bf16[4096,128]{1,0:T(8,128)(2,1)} %bitcast.33, bf16[768,4096]{1,0:T(8,128)(2,1)} %copy-done.1), kind=kOutput, calls=%fused_computation.3 | convolution fusion | flops 814743552 | bytes 13828096 | tf_op jit(solution)/shard_map/dot_general | solution.py:195
  123.1 0.0 copy-done.2
  123.1 1.5 %bitcast_convert_fusion = f32[4096,128]{1,0:T(8,128)} fusion(bf16[2,4,4,128,128]{4,3,2,1,0:T(8,128)(2,1)S(1)} %copy-done.2), kind=kLoop, calls=%fused_computation.15 | loop fusion | flops 524288 | bytes 3145728 | tf_op jit(solution)/shard_map/convert_element_type | solution.py:194
  (2 shorter events, 0.0 us)
Async XLA Ops:
  0.6 10.6 %copy-start = (bf16[4096,128]{1,0:T(8,128)(2,1)S(1)}, bf16[4096,128]{1,0:T(8,128)(2,1)}, u32[]{:S(2)}) copy-start(bf16[4096,128]{1,0:T(8,128)(2,1)} %param.7) | copy-start | bytes 3145732
  8.5 2.7 %copy-start.1 = (bf16[768,4096]{1,0:T(8,128)(2,1)}, bf16[768,4096]{1,0:T(8,128)(2,1)S(1)}, u32[]{:S(2)}) copy-start(bf16[768,4096]{1,0:T(8,128)(2,1)S(1)} %fusion) | copy-start | bytes 18874372
  115.4 7.7 %copy-start.2 = (bf16[2,4,4,128,128]{4,3,2,1,0:T(8,128)(2,1)S(1)}, bf16[2,4,4,128,128]{4,3,2,1,0:T(8,128)(2,1)}, u32[]{:S(2)}) copy-start(bf16[2,4,4,128,128]{4,3,2,1,0:T(8,128)(2,1)} %shard_map.60) | copy-start | bytes 3145732

commit v2 on v1

--- a/solution.py
+++ b/solution.py
@@ -172,9 +172,57 @@
     return out.reshape(width, rank)
 
 
-def orthonormal(p_rows, gram_matrix):
-    factor = jnp.linalg.cholesky(gram_matrix)
-    return jax.scipy.linalg.solve_triangular(factor, p_rows.T, lower=True).T.astype(jnp.bfloat16)
+def inverse_factor(gram_matrix, block):
+    rank = gram_matrix.shape[0]
+    row = lax.broadcasted_iota(jnp.int32, (rank, rank), 0)
+    col = lax.broadcasted_iota(jnp.int32, (rank, rank), 1)
+    left = gram_matrix
+    right = jnp.where(row == col, 1.0, 0.0).astype(jnp.float32)
+    sub = lax.broadcasted_iota(jnp.int32, (block, rank), 0)
+    done = []
+    for start in range(0, rank, block):
+        u, w = left[:block], right[:block]
+        cols = [jnp.broadcast_to(u[:, start + j:start + j + 1], (block, rank)) for j in range(block)]
+        scale = jnp.zeros((block, rank), jnp.float32)
+        for j in range(block):
+            pivot = cols[j][j:j + 1]
+            scale = jnp.where(sub == j, lax.rsqrt(pivot), scale)
+            m = jnp.where(sub > j, cols[j] * (1.0 / pivot), 0.0)
+            for i in range(j + 1, block):
+                cols[i] = cols[i] - m * cols[i][j:j + 1]
+            u = u - m * u[j:j + 1]
+            w = w - m * w[j:j + 1]
+        u, w = u * scale, w * scale
+        done.append(w)
+        if start + block < rank:
+            both = jnp.concatenate([u, w], axis=1)
+            update = lax.dot_general(
+                u, both, (((0,), (0,)), ((), ())), precision=lax.Precision.HIGHEST,
+                preferred_element_type=jnp.float32,
+            )[start + block:]
+            left = left[block:] - update[:, :rank]
+            right = right[block:] - update[:, rank:]
+    return jnp.concatenate(done, axis=0)
+
+
+def orthonormal_kernel(p_ref, out_ref):
+    p = p_ref[...]
+    gram_matrix = lax.dot_general(
+        p, p, (((0,), (0,)), ((), ())), precision=lax.Precision.HIGHEST, preferred_element_type=jnp.float32
+    )
+    inverse = inverse_factor(gram_matrix, 16)
+    out_ref[...] = lax.dot_general(
+        p, inverse, (((1,), (1,)), ((), ())), precision=lax.Precision.HIGHEST, preferred_element_type=jnp.float32
+    ).astype(out_ref.dtype)
+
+
+def orthonormal(p_rows):
+    return pl.pallas_call(
+        orthonormal_kernel,
+        out_shape=jax.ShapeDtypeStruct(p_rows.shape, jnp.bfloat16),
+        in_specs=[VMEM],
+        out_specs=VMEM,
+    )(p_rows)
 
 
 def shards(hidden_acts, out_grad, error_prev, right_prev):
@@ -185,8 +233,7 @@
     compensated = (weight_grad + error_prev[0].astype(jnp.float32)).astype(jnp.bfloat16)
     partial_value = jnp.dot(compensated, right_prev, preferred_element_type=jnp.float32)
     p_sum = left_sum(partial_value, replicas, tensors)
-    gram_matrix = jnp.dot(p_sum.T, p_sum, precision=lax.Precision.HIGHEST)
-    left_low = orthonormal(p_sum, gram_matrix)
+    left_low = orthonormal(p_sum)
     right_terms = lax.dot_general(
         compensated, left_low, (((0,), (0,)), ((), ())), preferred_element_type=jnp.float32
     )

time: 125 us -> 106 us (0.85)
  other arithmetic: 24.4 us -> 1.52 us
  Pallas kernels: 69.3 us -> 77 us
  matrix products: 27.4 us -> 24.1 us
    another operation x5 -> x0, other arithmetic: 22.9 us -> none  [the longest x3 12.4 us: orthonormal(): factor = jnp.linalg.cholesky(gram_matrix)]
    pallas_call x0 -> x1, Pallas kernels: none -> 7.68 us  [orthonormal(): pl.pallas_call(orthonormal_kernel, out_shape=jax.ShapeDtypeStruct(p_rows....]
    dot_general x1 -> x0, matrix products: 1.91 us -> none  [shards(): gram_matrix = jnp.dot(p_sum.T, p_sum, precision=lax.Precision.HIGHEST)]
    another operation x1 -> x0, matrix products: 1.46 us -> none  [orthonormal(): jax.scipy.linalg.solve_triangular(factor, p_rows.T, lower=True)]
    unnamed x6 -> x8, local copies, waits for them, and re-layouts: 2.71 us -> 2.72 us
where the time goes in v2:
time: 106 us
  Pallas kernels  77 us (73%)
  matrix products  24.1 us (23%)
  local copies, waits for them, and re-layouts  2.72 us (3%)
  other arithmetic  1.52 us (1%)
    pallas_call x1, Pallas kernels, right_mean(): pl.pallas_call(functools.partial(right_kernel, replicas, inner, chunks),...  44.5 us
    pallas_call x1, Pallas kernels, left_sum(): pl.pallas_call(functools.partial(left_kernel, replicas, tensors, piece),...  24.8 us
    dot_general x1, matrix products, shards(): lax.dot_general(out_grad, hidden_acts, (((0,), (0,)), ((), ())), preferre...  7.85 us
    dot_general x1, matrix products, shards(): lax.dot_general(left_low, right_low, (((1,), (1,)), ((), ())), preferred_...  7.7 us
    pallas_call x1, Pallas kernels, orthonormal(): pl.pallas_call(orthonormal_kernel, out_shape=jax.ShapeDtypeStruct(p_rows....  7.68 us
    dot_general x1, matrix products, shards(): lax.dot_general(compensated, left_low, (((0,), (0,)), ((), ())), preferre...  5.98 us
    unnamed x8, local copies, waits for them, and re-layouts  2.72 us
    dot_general x1, matrix products, shards(): jnp.dot(compensated, right_prev, preferred_element_type=jnp.float32)  2.53 us

profile of v2, /device:TPU:0, one launch (start us, length us, event | category | flops | bytes accessed | tf_op | source)
XLA Modules:
  0.0 106.0 jit_solution(2501574847807716843)
XLA Ops:
  0.6 0.0 copy-start
  0.6 7.8 %fusion = bf16[768,4096]{1,0:T(8,128)(2,1)S(1)} fusion(bf16[512,768]{1,0:T(8,128)(2,1)} %param.5, bf16[512,4096]{1,0:T(8,128)(2,1)} %param.4, bf16[1,768,4096]{2,1,0:T(8,128)(2,1)} %param.6), kind=kOutput, calls=%fused_computation.1 | convolution fusion | flops 3230662656 | bytes 17563648 | tf_op jit(solution)/shard_map/dot_general | solution.py:230
  8.5 0.0 copy-start.1
  8.5 2.7 %copy-done.1 = bf16[768,4096]{1,0:T(8,128)(2,1)} copy-done((bf16[768,4096]{1,0:T(8,128)(2,1)}, bf16[768,4096]{1,0:T(8,128)(2,1)S(1)}, u32[]{:S(2)}) %copy-start.1) | copy-done | bytes 6291480
  11.2 0.0 copy-done
  11.2 2.5 %fusion.2 = f32[768,128]{1,0:T(8,128)} fusion(bf16[768,4096]{1,0:T(8,128)(2,1)S(1)} %fusion, bf16[4096,128]{1,0:T(8,128)(2,1)S(1)} %copy-done), kind=kOutput, calls=%fused_computation.5 | convolution fusion | flops 805306368 | bytes 7733248 | tf_op jit(solution)/shard_map/dot_general | solution.py:234
  13.7 24.8 %shard_map.59 = f32[32,24,128]{2,1,0:T(8,128)} custom-call(f32[32,24,128]{2,1,0:T(8,128)} %bitcast.21), custom_call_target="tpu_custom_call" | custom-call | tf_op jit(solution)/shard_map/pallas_call | solution.py:68
  38.6 7.7 %shard_map.60 = bf16[768,128]{1,0:T(8,128)(2,1)} custom-call(f32[768,128]{1,0:T(8,128)} %bitcast.20), custom_call_target="tpu_custom_call" | custom-call | tf_op jit(solution)/shard_map/pallas_call | solution.py:220
  46.3 0.0 copy-start.3
  46.3 6.0 %fusion.3 = f32[4096,128]{1,0:T(8,128)} fusion(bf16[768,4096]{1,0:T(8,128)(2,1)} %copy-done.1, bf16[768,128]{1,0:T(8,128)(2,1)} %shard_map.60), kind=kOutput, calls=%fused_computation.6 | convolution fusion | flops 805306368 | bytes 8585216 | tf_op jit(solution)/shard_map/dot_general | solution.py:237
  52.2 44.5 %shard_map.61 = bf16[2,4,4,128,128]{4,3,2,1,0:T(8,128)(2,1)} custom-call(f32[2,4,4,128,128]{4,3,2,1,0:T(8,128)} %bitcast.18), custom_call_target="tpu_custom_call" | custom-call | tf_op jit(solution)/shard_map/pallas_call | solution.py:156
  96.7 0.0 copy-done.3
  96.7 0.0 copy-start.2
  96.8 7.7 %fusion.1 = bf16[1,768,4096]{2,1,0:T(8,128)(2,1)} fusion(bf16[768,128]{1,0:T(8,128)(2,1)S(1)} %copy-done.3, bf16[4096,128]{1,0:T(8,128)(2,1)} %bitcast.19, bf16[768,4096]{1,0:T(8,128)(2,1)} %copy-done.1), kind=kOutput, calls=%fused_computation.3 | convolution fusion | flops 814743552 | bytes 13828096 | tf_op jit(solution)/shard_map/dot_general | solution.py:242
  104.5 0.0 copy-done.2
  104.5 1.5 %bitcast_convert_fusion = f32[4096,128]{1,0:T(8,128)} fusion(bf16[2,4,4,128,128]{4,3,2,1,0:T(8,128)(2,1)S(1)} %copy-done.2), kind=kLoop, calls=%fused_computation.4 | loop fusion | flops 524288 | bytes 3145728 | tf_op jit(solution)/shard_map/convert_element_type | solution.py:241
Async XLA Ops:
  0.6 10.6 %copy-start = (bf16[4096,128]{1,0:T(8,128)(2,1)S(1)}, bf16[4096,128]{1,0:T(8,128)(2,1)}, u32[]{:S(2)}) copy-start(bf16[4096,128]{1,0:T(8,128)(2,1)} %param.7) | copy-start | bytes 3145732
  8.5 2.7 %copy-start.1 = (bf16[768,4096]{1,0:T(8,128)(2,1)}, bf16[768,4096]{1,0:T(8,128)(2,1)S(1)}, u32[]{:S(2)}) copy-start(bf16[768,4096]{1,0:T(8,128)(2,1)S(1)} %fusion) | copy-start | bytes 18874372
  46.3 50.5 %copy-start.3 = (bf16[768,128]{1,0:T(8,128)(2,1)S(1)}, bf16[768,128]{1,0:T(8,128)(2,1)}, u32[]{:S(2)}) copy-start(bf16[768,128]{1,0:T(8,128)(2,1)} %shard_map.60) | copy-start | bytes 589828
  96.7 7.7 %copy-start.2 = (bf16[2,4,4,128,128]{4,3,2,1,0:T(8,128)(2,1)S(1)}, bf16[2,4,4,128,128]{4,3,2,1,0:T(8,128)(2,1)}, u32[]{:S(2)}) copy-start(bf16[2,4,4,128,128]{4,3,2,1,0:T(8,128)(2,1)} %shard_map.61) | copy-start | bytes 3145732

commit v3 on v2

--- a/solution.py
+++ b/solution.py
@@ -81,14 +81,33 @@
     return out.reshape(count * piece, rank)[:rows]
 
 
-def right_kernel(replicas, inner, chunks, x_ref, out_ref, sendx, recvx, sendz, recvz, final, gathz, gathx,
-                 sx, rx, sz, rz, sg, rg, sh, rh):
+def right_kernel(replicas, inner, chunks, rows, comp_hbm, left_ref, out_ref, comp, sendx, recvx, own, sendz, recvz,
+                 final, gathz, gathx, load, sx, rx, sz, rz, sg, rg, sh, rh):
     outer = replicas // inner
+    rank = left_ref.shape[1]
+    slab = outer * rows
     me = lax.axis_index("replica")
     mz, mx = me // inner, lax.rem(me, inner)
     px = lax.rem(mx + 1, inner)
     partner = {"replica": mz * inner + px}
 
+    def fetch(side, c):
+        start = pl.multiple_of((side * chunks + c) * slab, slab)
+        place = c if side is px else chunks + c
+        return pltpu.make_async_copy(comp_hbm.at[:, pl.ds(start, slab)], comp.at[place], load.at[place])
+
+    for c in range(chunks):
+        fetch(px, c).start()
+    for c in range(chunks):
+        fetch(mx, c).start()
+
+    def terms(side, c):
+        fetch(side, c).wait()
+        place = c if side is px else chunks + c
+        return lax.dot_general(
+            comp[place], left_ref[...], (((0,), (0,)), ((), ())), preferred_element_type=jnp.float32
+        ).reshape(outer, rows, rank)
+
     def zpeer(k):
         oz = lax.rem(mz + k, outer)
         return oz, {"replica": oz * inner + mx}
@@ -97,28 +116,31 @@
     pl.semaphore_signal(barrier, inc=1, device_id=partner, device_id_type=MESH)
     for k in range(1, outer):
         pl.semaphore_signal(barrier, inc=1, device_id=zpeer(k)[1], device_id_type=MESH)
-    pl.semaphore_wait(barrier, outer)
-
-    for c in range(chunks):
-        sendx[c] = x_ref[px, :, c].astype(jnp.bfloat16)
-        if True:
-            pltpu.make_async_remote_copy(
-                src_ref=sendx.at[c], dst_ref=recvx.at[c], send_sem=sx.at[c], recv_sem=rx.at[c],
-                device_id=partner, device_id_type=MESH,
-            ).start()
-    for c in range(chunks):
+
+    def pair_scatter(c):
+        sendx[c] = terms(px, c).astype(jnp.bfloat16)
+        if c == 0:
+            pl.semaphore_wait(barrier, outer)
+        pltpu.make_async_remote_copy(
+            src_ref=sendx.at[c], dst_ref=recvx.at[c], send_sem=sx.at[c], recv_sem=rx.at[c],
+            device_id=partner, device_id_type=MESH,
+        ).start()
+
+    def line_scatter(c):
+        mine = terms(mx, c)
         wait_bytes(recvx.at[c], rx.at[c])
-        sendz[c] = (x_ref[mx, :, c] + recvx[c].astype(jnp.float32)).astype(jnp.bfloat16)
+        own[c] = mine + recvx[c].astype(jnp.float32)
+        sendz[c] = own[c].astype(jnp.bfloat16)
         for k in range(1, outer):
             oz, where = zpeer(k)
             pltpu.make_async_remote_copy(
                 src_ref=sendz.at[c, oz], dst_ref=recvz.at[c, k - 1], send_sem=sz.at[c], recv_sem=rz.at[c],
                 device_id=where, device_id_type=MESH,
             ).start()
-    for c in range(chunks):
+
+    def line_gather(c):
         wait_bytes(recvz.at[c], rz.at[c])
-        own = x_ref[mx, mz, c] + recvx[c, mz].astype(jnp.float32)
-        total = own + jnp.sum(recvz[c].astype(jnp.float32), axis=0)
+        total = own[c, mz] + jnp.sum(recvz[c].astype(jnp.float32), axis=0)
         final[c] = (total / replicas).astype(jnp.bfloat16)
         for k in range(1, outer):
             oz, where = zpeer(k)
@@ -127,16 +149,28 @@
                 device_id=where, device_id_type=MESH,
             ).start()
         gathz[c, mz] = final[c]
-    for c in range(chunks):
+
+    def pair_gather(c):
         wait_bytes(recvz.at[c], rg.at[c])
         pltpu.make_async_remote_copy(
             src_ref=gathz.at[c], dst_ref=gathx.at[c], send_sem=sh.at[c], recv_sem=rh.at[c],
             device_id=partner, device_id_type=MESH,
         ).start()
-        out_ref[mx, :, c] = gathz[c]
+        out_ref[mx, c] = gathz[c]
+
+    for c in range(chunks):
+        pair_scatter(c)
+    lag = 3
+    for step in range(chunks + 2 * lag):
+        if step < chunks:
+            line_scatter(step)
+        if 0 <= step - lag < chunks:
+            line_gather(step - lag)
+        if 0 <= step - 2 * lag < chunks:
+            pair_gather(step - 2 * lag)
     for c in range(chunks):
         wait_bytes(gathx.at[c], rh.at[c])
-        out_ref[px, :, c] = gathx[c]
+        out_ref[px, c] = gathx[c]
     for c in range(chunks):
         wait_bytes(sendx.at[c], sx.at[c])
         wait_bytes(recvz.at[c], sz.at[c])
@@ -144,31 +178,35 @@
         wait_bytes(gathz.at[c], sh.at[c])
 
 
-def right_mean(terms, replicas):
-    width, rank = terms.shape
+def right_mean(compensated, left_low, replicas):
+    depth, width = compensated.shape
+    rank = left_low.shape[1]
     inner = 2
     outer = replicas // inner
-    rows = width // replicas
-    chunks = next(c for c in (4, 2, 1) if rows % (c * 16) == 0)
-    rows //= chunks
-    shape = (inner, outer, chunks, rows, rank)
+    piece = width // replicas
+    chunks = next(c for c in (8, 4, 2, 1) if piece % (c * 16) == 0 and (width // inner // c) % 128 == 0)
+    rows = piece // chunks
     bf = jnp.bfloat16
+    whole = pltpu.VMEM((chunks, outer, rows, rank), bf)
     out = pl.pallas_call(
-        functools.partial(right_kernel, replicas, inner, chunks),
-        out_shape=jax.ShapeDtypeStruct(shape, bf),
-        in_specs=[VMEM],
+        functools.partial(right_kernel, replicas, inner, chunks, rows),
+        out_shape=jax.ShapeDtypeStruct((inner, chunks, outer, rows, rank), bf),
+        in_specs=[pl.BlockSpec(memory_space=pl.ANY), VMEM],
         out_specs=VMEM,
         scratch_shapes=[
-            pltpu.VMEM((chunks, outer, rows, rank), bf),
-            pltpu.VMEM((chunks, outer, rows, rank), bf),
-            pltpu.VMEM((chunks, outer, rows, rank), bf),
+            pltpu.VMEM((inner * chunks, depth, outer * rows), bf),
+            whole,
+            whole,
+            pltpu.VMEM((chunks, outer, rows, rank), jnp.float32),
+            whole,
             pltpu.VMEM((chunks, outer - 1, rows, rank), bf),
             pltpu.VMEM((chunks, rows, rank), bf),
-            pltpu.VMEM((chunks, outer, rows, rank), bf),
-            pltpu.VMEM((chunks, outer, rows, rank), bf),
+            whole,
+            whole,
+            pltpu.SemaphoreType.DMA((inner * chunks,)),
         ] + [pltpu.SemaphoreType.DMA((chunks,))] * 8,
         compiler_params=pltpu.CompilerParams(collective_id=1, has_side_effects=True),
-    )(terms.reshape(shape))
+    )(compensated, left_low)
     return out.reshape(width, rank)
 
 
@@ -234,10 +272,7 @@
     partial_value = jnp.dot(compensated, right_prev, preferred_element_type=jnp.float32)
     p_sum = left_sum(partial_value, replicas, tensors)
     left_low = orthonormal(p_sum)
-    right_terms = lax.dot_general(
-        compensated, left_low, (((0,), (0,)), ((), ())), preferred_element_type=jnp.float32
-    )
-    right_low = right_mean(right_terms, replicas)
+    right_low = right_mean(compensated, left_low, replicas)
     right_next = right_low.astype(jnp.float32)
     approx = lax.dot_general(
         left_low, right_low, (((1,), (1,)), ((), ())), preferred_element_type=jnp.float32

time: 106 us -> 97 us (0.915)
  matrix products: 24.1 us -> 18.1 us
  Pallas kernels: 77 us -> 73.8 us
    dot_general x1 -> x0, matrix products: 5.98 us -> none  [shards(): lax.dot_general(compensated, left_low, (((0,), (0,)), ((), ())), preferre...]
    pallas_call x1, Pallas kernels: 44.5 us -> 41.3 us  [right_mean(): pl.pallas_call(functools.partial(right_kernel, replicas, inner, chunks, r...]
where the time goes in v3:
time: 97 us; the launch traced here: 96.8 us
  Pallas kernels  73.8 us (76%)
  matrix products  18.1 us (19%)
  local copies, waits for them, and re-layouts  2.72 us (3%)
  other arithmetic  1.52 us (2%)
    pallas_call x1, Pallas kernels, right_mean(): pl.pallas_call(functools.partial(right_kernel, replicas, inner, chunks, r...  41.3 us
    pallas_call x1, Pallas kernels, left_sum(): pl.pallas_call(functools.partial(left_kernel, replicas, tensors, piece),...  24.8 us
    dot_general x1, matrix products, shards(): lax.dot_general(out_grad, hidden_acts, (((0,), (0,)), ((), ())), preferre...  7.85 us
    dot_general x1, matrix products, shards(): lax.dot_general(left_low, right_low, (((1,), (1,)), ((), ())), preferred_...  7.7 us
    pallas_call x1, Pallas kernels, orthonormal(): pl.pallas_call(orthonormal_kernel, out_shape=jax.ShapeDtypeStruct(p_rows....  7.67 us
    unnamed x8, local copies, waits for them, and re-layouts  2.72 us
    dot_general x1, matrix products, shards(): jnp.dot(compensated, right_prev, preferred_element_type=jnp.float32)  2.53 us

profile of v3, /device:TPU:0, one launch (start us, length us, event | category | flops | bytes accessed | tf_op | source)
XLA Modules:
  0.0 96.8 jit_solution(16685160980476719034)
XLA Ops:
  0.6 0.0 copy-start
  0.6 7.8 %fusion.comp_hbm = bf16[768,4096]{1,0:T(8,128)(2,1)S(1)} fusion(bf16[512,768]{1,0:T(8,128)(2,1)} %param.5, bf16[512,4096]{1,0:T(8,128)(2,1)} %param.4, bf16[1,768,4096]{2,1,0:T(8,128)(2,1)} %param.6), kind=kOutput, calls=%fused_computation.1 | convolution fusion | flops 3230662656 | bytes 17563648 | tf_op jit(solution)/shard_map/dot_general | solution.py:268
  8.5 0.0 copy-start.1
  8.5 2.7 %copy-done.1 = bf16[768,4096]{1,0:T(8,128)(2,1)} copy-done((bf16[768,4096]{1,0:T(8,128)(2,1)}, bf16[768,4096]{1,0:T(8,128)(2,1)S(1)}, u32[]{:S(2)}) %copy-start.1) | copy-done | bytes 6291480
  11.2 0.0 copy-done
  11.2 2.5 %fusion.2 = f32[768,128]{1,0:T(8,128)} fusion(bf16[768,4096]{1,0:T(8,128)(2,1)S(1)} %fusion.comp_hbm, bf16[4096,128]{1,0:T(8,128)(2,1)S(1)} %copy-done), kind=kOutput, calls=%fused_computation.5 | convolution fusion | flops 805306368 | bytes 7733248 | tf_op jit(solution)/shard_map/dot_general | solution.py:272
  13.7 24.8 %shard_map.59 = f32[32,24,128]{2,1,0:T(8,128)} custom-call(f32[32,24,128]{2,1,0:T(8,128)} %bitcast.17), custom_call_target="tpu_custom_call" | custom-call | tf_op jit(solution)/shard_map/pallas_call | solution.py:68
  38.6 7.7 %shard_map.60.left_ref = bf16[768,128]{1,0:T(8,128)(2,1)} custom-call(f32[768,128]{1,0:T(8,128)} %bitcast.16), custom_call_target="tpu_custom_call" | custom-call | tf_op jit(solution)/shard_map/pallas_call | solution.py:258
  46.3 0.0 copy-start.3
  46.3 41.3 %shard_map.61 = bf16[2,8,4,64,128]{4,3,2,1,0:T(8,128)(2,1)} custom-call(bf16[768,4096]{1,0:T(8,128)(2,1)} %copy-done.1, bf16[768,128]{1,0:T(8,128)(2,1)} %shard_map.60.left_ref), custom_call_target="tpu_custom_call" | custom-call | tf_op jit(solution)/shard_map/pallas_call | solution.py:191
  87.6 0.0 copy-done.3
  87.6 0.0 copy-start.2
  87.6 7.7 %fusion.1 = bf16[1,768,4096]{2,1,0:T(8,128)(2,1)} fusion(bf16[768,128]{1,0:T(8,128)(2,1)S(1)} %copy-done.3, bf16[4096,128]{1,0:T(8,128)(2,1)} %bitcast.15, bf16[768,4096]{1,0:T(8,128)(2,1)} %copy-done.1), kind=kOutput, calls=%fused_computation.3 | convolution fusion | flops 814743552 | bytes 13828096 | tf_op jit(solution)/shard_map/dot_general | solution.py:277
  95.3 0.0 copy-done.2
  95.3 1.5 %bitcast_convert_fusion = f32[4096,128]{1,0:T(8,128)} fusion(bf16[2,8,4,64,128]{4,3,2,1,0:T(8,128)(2,1)S(1)} %copy-done.2), kind=kLoop, calls=%fused_computation.4 | loop fusion | flops 524288 | bytes 3145728 | tf_op jit(solution)/shard_map/convert_element_type | solution.py:276
Async XLA Ops:
  0.6 10.6 %copy-start = (bf16[4096,128]{1,0:T(8,128)(2,1)S(1)}, bf16[4096,128]{1,0:T(8,128)(2,1)}, u32[]{:S(2)}) copy-start(bf16[4096,128]{1,0:T(8,128)(2,1)} %param.7) | copy-start | bytes 3145732
  8.5 2.7 %copy-start.1 = (bf16[768,4096]{1,0:T(8,128)(2,1)}, bf16[768,4096]{1,0:T(8,128)(2,1)S(1)}, u32[]{:S(2)}) copy-start(bf16[768,4096]{1,0:T(8,128)(2,1)S(1)} %fusion.comp_hbm) | copy-start | bytes 18874372
  46.3 41.3 %copy-start.3 = (bf16[768,128]{1,0:T(8,128)(2,1)S(1)}, bf16[768,128]{1,0:T(8,128)(2,1)}, u32[]{:S(2)}) copy-start(bf16[768,128]{1,0:T(8,128)(2,1)} %shard_map.60.left_ref) | copy-start | bytes 589828
  87.6 7.7 %copy-start.2 = (bf16[2,8,4,64,128]{4,3,2,1,0:T(8,128)(2,1)S(1)}, bf16[2,8,4,64,128]{4,3,2,1,0:T(8,128)(2,1)}, u32[]{:S(2)}) copy-start(bf16[2,8,4,64,128]{4,3,2,1,0:T(8,128)(2,1)} %shard_map.61) | copy-start | bytes 3145732

commit v4 on v3

--- a/solution.py
+++ b/solution.py
@@ -15,70 +15,171 @@
     pltpu.make_async_copy(view, view, sem).wait()
 
 
-def left_kernel(replicas, tensors, piece, x_ref, out_ref, recv, mine, gathered, send_sem, recv_sem, send2_sem, recv2_sem):
-    count = replicas * tensors
-    me = lax.axis_index("replica") * tensors + lax.axis_index("tensor")
+def left_kernel(replicas, tensors, chunks, tiles, used, act_hbm, cot_hbm, err_hbm, right_hbm, comp_hbm, out_ref,
+                act, cot, err, right, comp, part, half, recvc, recv, mine, gathered, other,
+                act_sem, cot_sem, err_sem, right_sem, comp_sem, sc, rc, ss, rs, sg, rg, sh, rh):
+    lines = tensors // 2
+    peers = replicas * lines
+    rows = cot.shape[1] // chunks
+    width = act.shape[2]
+    replica, tensor = lax.axis_index("replica"), lax.axis_index("tensor")
+    core = lax.rem(tensor, 2)
+    mate = 1 - core
+    partner = (replica, tensor - core + mate)
+    me = replica * lines + tensor // 2
 
     def peer(k):
-        other = lax.rem(me + k, count)
-        return other, (other // tensors, lax.rem(other, tensors))
+        q = lax.rem(me + k, peers)
+        return q, (q // lines, lax.rem(q, lines) * 2 + core)
+
+    def err_copy(c, t):
+        return pltpu.make_async_copy(
+            err_hbm.at[0, pl.ds(c * rows, rows), pl.ds(t * width, width)], err.at[c, t], err_sem.at[c, t])
+
+    def comp_copy(c, t):
+        return pltpu.make_async_copy(
+            comp.at[c, t], comp_hbm.at[pl.ds(c * rows, rows), pl.ds(t * width, width)], comp_sem.at[c, t])
+
+    def act_copy(t):
+        return pltpu.make_async_copy(act_hbm.at[:, pl.ds(t * width, width)], act.at[t], act_sem.at[t])
+
+    def right_copy(t):
+        return pltpu.make_async_copy(right_hbm.at[pl.ds(t * width, width)], right.at[t], right_sem.at[t])
+
+    pltpu.make_async_copy(cot_hbm, cot, cot_sem).start()
+    for t in range(tiles):
+        act_copy(t).start()
+        err_copy(0, t).start()
+        right_copy(t).start()
+    for c in range(1, chunks):
+        for t in range(tiles):
+            err_copy(c, t).start()
 
     barrier = pltpu.get_barrier_semaphore()
+    pl.semaphore_signal(barrier, inc=1, device_id=partner, device_id_type=MESH)
 
     def greet(k, carry):
         pl.semaphore_signal(barrier, inc=1, device_id=peer(k)[1], device_id_type=MESH)
         return carry
 
-    lax.fori_loop(1, count, greet, 0)
-    pl.semaphore_wait(barrier, count - 1)
-
-    def scatter(k, carry):
-        other, where = peer(k)
+    lax.fori_loop(1, peers, greet, 0)
+
+    def core_copy(c):
+        return pltpu.make_async_remote_copy(
+            src_ref=part.at[c, mate], dst_ref=recvc.at[c], send_sem=sc.at[c], recv_sem=rc.at[c],
+            device_id=partner, device_id_type=MESH,
+        )
+
+    def scatter_chunk(c):
+        wait_bytes(recvc.at[c], rc.at[c])
+        half[c, :used] = (part[c, core] + recvc[c]).reshape(half[c, :used].shape)
+        if used < peers:
+            half[c, used:] = jnp.zeros_like(half[c, used:])
+
+        def scatter(k, carry):
+            q, where = peer(k)
+            pltpu.make_async_remote_copy(
+                src_ref=half.at[c, q], dst_ref=recv.at[k - 1, c], send_sem=ss, recv_sem=rs,
+                device_id=where, device_id_type=MESH,
+            ).start()
+            return carry
+
+        lax.fori_loop(1, peers, scatter, 0)
+
+    for c in range(chunks):
+        total = jnp.zeros((rows, right.shape[2]), jnp.float32)
+        for t in range(tiles):
+            if c == 0:
+                if t == 0:
+                    pltpu.make_async_copy(cot_hbm, cot, cot_sem).wait()
+                act_copy(t).wait()
+                right_copy(t).wait()
+            err_copy(c, t).wait()
+            grad = lax.dot_general(
+                cot[:, c * rows:(c + 1) * rows], act[t], (((0,), (0,)), ((), ())),
+                preferred_element_type=jnp.float32,
+            )
+            compensated = (grad + err[c, t].astype(jnp.float32)).astype(jnp.bfloat16)
+            comp[c, t] = compensated
+            comp_copy(c, t).start()
+            total = total + jnp.dot(compensated, right[t], preferred_element_type=jnp.float32)
+        part[c] = total.reshape(part.shape[1:])
+        if c == 0:
+            pl.semaphore_wait(barrier, peers)
+        core_copy(c).start()
+        if c:
+            scatter_chunk(c - 1)
+    scatter_chunk(chunks - 1)
+
+    wait_bytes(recv, rs)
+    mine[...] = half[:, me] + jnp.sum(recv[...], axis=0)
+
+    def gather(k, carry):
+        q, where = peer(k)
         pltpu.make_async_remote_copy(
-            src_ref=x_ref.at[other], dst_ref=recv.at[k - 1], send_sem=send_sem, recv_sem=recv_sem,
+            src_ref=mine, dst_ref=gathered.at[me], send_sem=sg, recv_sem=rg,
             device_id=where, device_id_type=MESH,
         ).start()
         return carry
 
-    lax.fori_loop(1, count, scatter, 0)
-    wait_bytes(recv, recv_sem)
-    mine[...] = x_ref[me] + jnp.sum(recv[...], axis=0)
-
-    def gather(k, carry):
-        other, where = peer(k)
-        pltpu.make_async_remote_copy(
-            src_ref=mine, dst_ref=gathered.at[me], send_sem=send2_sem, recv_sem=recv2_sem,
-            device_id=where, device_id_type=MESH,
-        ).start()
-        return carry
-
-    lax.fori_loop(1, count, gather, 0)
+    lax.fori_loop(1, peers, gather, 0)
     gathered[me] = mine[...]
-    wait_bytes(recv, recv2_sem)
-    out_ref[...] = gathered[...]
-    wait_bytes(recv, send_sem)
-    wait_bytes(recv, send2_sem)
-
-
-def left_sum(partial_value, replicas, tensors):
-    rows, rank = partial_value.shape
-    count = replicas * tensors
-    piece = -(-rows // (count * 8)) * 8
-    padded = jnp.pad(partial_value, ((0, count * piece - rows), (0, 0))).reshape(count, piece, rank)
-    out = pl.pallas_call(
-        functools.partial(left_kernel, replicas, tensors, piece),
-        out_shape=jax.ShapeDtypeStruct((count, piece, rank), jnp.float32),
-        in_specs=[VMEM],
-        out_specs=VMEM,
+    wait_bytes(recv, rg)
+    pltpu.make_async_remote_copy(
+        src_ref=gathered, dst_ref=other, send_sem=sh, recv_sem=rh, device_id=partner, device_id_type=MESH,
+    ).start()
+    for c in range(chunks):
+        out_ref[c, core] = gathered[:used, c]
+    wait_bytes(other, rh)
+    for c in range(chunks):
+        out_ref[c, mate] = other[:used, c]
+    for c in range(chunks):
+        wait_bytes(part.at[c, mate], sc.at[c])
+        for t in range(tiles):
+            comp_copy(c, t).wait()
+    wait_bytes(recv, ss)
+    wait_bytes(recv, sg)
+    wait_bytes(gathered, sh)
+
+
+def left_sum(hidden_acts, out_grad, error_prev, right_prev, replicas, tensors):
+    tokens, depth = out_grad.shape
+    columns, rank = right_prev.shape
+    peers = replicas * tensors // 2
+    chunks = next(c for c in (3, 2, 1) if depth % (c * 256) == 0)
+    tiles = next(t for t in (4, 2, 1) if columns % (t * 128) == 0)
+    rows, width = depth // chunks, columns // tiles
+    piece = -(-rows // (2 * peers * 8)) * 8
+    used = rows // (2 * piece)
+    bf, f32, dma = jnp.bfloat16, jnp.float32, pltpu.SemaphoreType.DMA
+    hbm = pl.BlockSpec(memory_space=pl.ANY)
+    compensated, p_sum = pl.pallas_call(
+        functools.partial(left_kernel, replicas, tensors, chunks, tiles, used),
+        out_shape=(
+            jax.ShapeDtypeStruct((depth, columns), bf),
+            jax.ShapeDtypeStruct((chunks, 2, used, piece, rank), f32),
+        ),
+        in_specs=[hbm] * 4,
+        out_specs=(hbm, VMEM),
         scratch_shapes=[
-            pltpu.VMEM((count - 1, piece, rank), jnp.float32),
-            pltpu.VMEM((piece, rank), jnp.float32),
-            pltpu.VMEM((count, piece, rank), jnp.float32),
-            pltpu.SemaphoreType.DMA, pltpu.SemaphoreType.DMA, pltpu.SemaphoreType.DMA, pltpu.SemaphoreType.DMA,
+            pltpu.VMEM((tiles, tokens, width), bf),
+            pltpu.VMEM((tokens, depth), bf),
+            pltpu.VMEM((chunks, tiles, rows, width), bf),
+            pltpu.VMEM((tiles, width, rank), bf),
+            pltpu.VMEM((chunks, tiles, rows, width), bf),
+            pltpu.VMEM((chunks, 2, rows // 2, rank), f32),
+            pltpu.VMEM((chunks, peers, piece, rank), f32),
+            pltpu.VMEM((chunks, rows // 2, rank), f32),
+            pltpu.VMEM((peers - 1, chunks, piece, rank), f32),
+            pltpu.VMEM((chunks, piece, rank), f32),
+            pltpu.VMEM((peers, chunks, piece, rank), f32),
+            pltpu.VMEM((peers, chunks, piece, rank), f32),
+            dma((tiles,)), dma, dma((chunks, tiles)), dma((tiles,)), dma((chunks, tiles)),
+            dma((chunks,)), dma((chunks,)), dma, dma, dma, dma, dma, dma,
         ],
         compiler_params=pltpu.CompilerParams(collective_id=0, has_side_effects=True),
-    )(padded)
-    return out.reshape(count * piece, rank)[:rows]
+    )(hidden_acts, out_grad, error_prev, right_prev)
+    return compensated, p_sum.reshape(depth, rank)
 
 
 def right_kernel(replicas, inner, chunks, rows, comp_hbm, left_ref, out_ref, comp, sendx, recvx, own, sendz, recvz,
@@ -265,12 +366,7 @@
 
 def shards(hidden_acts, out_grad, error_prev, right_prev):
     replicas, tensors = lax.axis_size("replica"), lax.axis_size("tensor")
-    weight_grad = lax.dot_general(
-        out_grad, hidden_acts, (((0,), (0,)), ((), ())), preferred_element_type=jnp.float32
-    )
-    compensated = (weight_grad + error_prev[0].astype(jnp.float32)).astype(jnp.bfloat16)
-    partial_value = jnp.dot(compensated, right_prev, preferred_element_type=jnp.float32)
-    p_sum = left_sum(partial_value, replicas, tensors)
+    compensated, p_sum = left_sum(hidden_acts, out_grad, error_prev, right_prev, replicas, tensors)
     left_low = orthonormal(p_sum)
     right_low = right_mean(compensated, left_low, replicas)
     right_next = right_low.astype(jnp.float32)

time: 97 us -> 84 us (0.87)
  matrix products: 18.1 us -> 7.69 us
  local copies, waits for them, and re-layouts: 2.72 us -> 0.01 us
    dot_general x2 -> x0, matrix products: 10.4 us -> none  [the longest x1 7.85 us: shards(): lax.dot_general(out_grad, hidden_acts, (((0,), (0,)), ((), ())), preferre...]
    pallas_call x1, Pallas kernels: 24.8 us -> 27.7 us  [left_sum(): pl.pallas_call(functools.partial(left_kernel, replicas, tensors, chunks,...]
    pallas_call x1, Pallas kernels: 41.3 us -> 38.5 us  [right_mean(): pl.pallas_call(functools.partial(right_kernel, replicas, inner, chunks, r...]
    unnamed x8 -> x4, local copies, waits for them, and re-layouts: 2.72 us -> 0.01 us
where the time goes in v4:
time: 84 us; the launch traced here: 83.8 us
  Pallas kernels  73.9 us (88%)
  matrix products  7.69 us (9%)
  other arithmetic  1.52 us (2%)
    pallas_call x1, Pallas kernels, right_mean(): pl.pallas_call(functools.partial(right_kernel, replicas, inner, chunks, r...  38.5 us
    pallas_call x1, Pallas kernels, left_sum(): pl.pallas_call(functools.partial(left_kernel, replicas, tensors, chunks,...  27.7 us
    dot_general x1, matrix products, shards(): lax.dot_general(left_low, right_low, (((1,), (1,)), ((), ())), preferred_...  7.69 us
    pallas_call x1, Pallas kernels, orthonormal(): pl.pallas_call(orthonormal_kernel, out_shape=jax.ShapeDtypeStruct(p_rows....  7.68 us

profile of v4, /device:TPU:0, one launch (start us, length us, event | category | flops | bytes accessed | tf_op | source)
XLA Modules:
  0.0 83.8 jit_solution(269401921999639639)
XLA Ops:
  0.6 27.7 %shard_map.59 = (bf16[768,4096]{1,0:T(8,128)(2,1)}, f32[3,2,16,8,128]{4,3,2,1,0:T(8,128)}) custom-call(bf16[512,4096]{1,0:T(8,128)(2,1)} %act_hbm.1, bf16[512,768]{1,0:T(8,128)(2,1)} %cot_hbm.1, bf16[1,768,4096]{2,1,0:T(8,128)(2,1)} %err_hbm.1, bf16[4096,128]{1,0:T(8,128)(2,1)} %right_hbm.1), custom_call_target="tpu_custom_call" | custom-call | tf_op jit(solution)/shard_map/pallas_call | solution.py:156
  28.4 7.7 %shard_map.60.left_ref = bf16[768,128]{1,0:T(8,128)(2,1)} custom-call(f32[768,128]{1,0:T(8,128)} %bitcast.8), custom_call_target="tpu_custom_call" | custom-call | tf_op jit(solution)/shard_map/pallas_call | solution.py:359
  36.0 0.0 copy-start.1
  36.0 38.5 %shard_map.61 = bf16[2,8,4,64,128]{4,3,2,1,0:T(8,128)(2,1)} custom-call(bf16[768,4096]{1,0:T(8,128)(2,1)} %get-tuple-element.4.comp_hbm, bf16[768,128]{1,0:T(8,128)(2,1)} %shard_map.60.left_ref), custom_call_target="tpu_custom_call" | custom-call | tf_op jit(solution)/shard_map/pallas_call | solution.py:292
  74.5 0.0 copy-done.1
  74.6 0.0 copy-start
  74.6 7.7 %fusion = bf16[1,768,4096]{2,1,0:T(8,128)(2,1)} fusion(bf16[768,128]{1,0:T(8,128)(2,1)S(1)} %copy-done.1, bf16[4096,128]{1,0:T(8,128)(2,1)} %bitcast.7, bf16[768,4096]{1,0:T(8,128)(2,1)} %get-tuple-element.4.comp_hbm), kind=kOutput, calls=%fused_computation.1 | convolution fusion | flops 814743552 | bytes 13828096 | tf_op jit(solution)/shard_map/dot_general | solution.py:373
  82.3 0.0 copy-done
  82.3 1.5 %bitcast_convert_fusion = f32[4096,128]{1,0:T(8,128)} fusion(bf16[2,8,4,64,128]{4,3,2,1,0:T(8,128)(2,1)S(1)} %copy-done), kind=kLoop, calls=%fused_computation.2 | loop fusion | flops 524288 | bytes 3145728 | tf_op jit(solution)/shard_map/convert_element_type | solution.py:372
Async XLA Ops:
  36.0 38.5 %copy-start.1 = (bf16[768,128]{1,0:T(8,128)(2,1)S(1)}, bf16[768,128]{1,0:T(8,128)(2,1)}, u32[]{:S(2)}) copy-start(bf16[768,128]{1,0:T(8,128)(2,1)} %shard_map.60.left_ref) | copy-start | bytes 589828
  74.6 7.7 %copy-start = (bf16[2,8,4,64,128]{4,3,2,1,0:T(8,128)(2,1)S(1)}, bf16[2,8,4,64,128]{4,3,2,1,0:T(8,128)(2,1)}, u32[]{:S(2)}) copy-start(bf16[2,8,4,64,128]{4,3,2,1,0:T(8,128)(2,1)} %shard_map.61) | copy-start | bytes 3145732

commit v5 on v4

--- a/solution.py
+++ b/solution.py
@@ -177,7 +177,7 @@
             dma((tiles,)), dma, dma((chunks, tiles)), dma((tiles,)), dma((chunks, tiles)),
             dma((chunks,)), dma((chunks,)), dma, dma, dma, dma, dma, dma,
         ],
-        compiler_params=pltpu.CompilerParams(collective_id=0, has_side_effects=True),
+        compiler_params=pltpu.CompilerParams(collective_id=0, has_side_effects=True, vmem_limit_bytes=60 * 1024 * 1024),
     )(hidden_acts, out_grad, error_prev, right_prev)
     return compensated, p_sum.reshape(depth, rank)
 
@@ -261,7 +261,7 @@
 
     for c in range(chunks):
         pair_scatter(c)
-    lag = 3
+    lag = 4
     for step in range(chunks + 2 * lag):
         if step < chunks:
             line_scatter(step)
@@ -306,7 +306,7 @@
             whole,
             pltpu.SemaphoreType.DMA((inner * chunks,)),
         ] + [pltpu.SemaphoreType.DMA((chunks,))] * 8,
-        compiler_params=pltpu.CompilerParams(collective_id=1, has_side_effects=True),
+        compiler_params=pltpu.CompilerParams(collective_id=1, has_side_effects=True, vmem_limit_bytes=54 * 1024 * 1024),
     )(compensated, left_low)
     return out.reshape(width, rank)
 
@@ -349,7 +349,7 @@
     gram_matrix = lax.dot_general(
         p, p, (((0,), (0,)), ((), ())), precision=lax.Precision.HIGHEST, preferred_element_type=jnp.float32
     )
-    inverse = inverse_factor(gram_matrix, 16)
+    inverse = inverse_factor(gram_matrix, 32)
     out_ref[...] = lax.dot_general(
         p, inverse, (((1,), (1,)), ((), ())), precision=lax.Precision.HIGHEST, preferred_element_type=jnp.float32
     ).astype(out_ref.dtype)
@@ -361,6 +361,7 @@
         out_shape=jax.ShapeDtypeStruct(p_rows.shape, jnp.bfloat16),
         in_specs=[VMEM],
         out_specs=VMEM,
+        compiler_params=pltpu.CompilerParams(vmem_limit_bytes=16 * 1024 * 1024),
     )(p_rows)
 
 

time: 84 us -> 82.2 us (0.979)
  matrix products: 7.69 us -> 5.91 us
  Pallas kernels: 73.9 us -> 72.2 us
  local copies, waits for them, and re-layouts: 0.01 us -> 1.67 us
    pallas_call x1, Pallas kernels: 7.68 us -> 5.34 us  [orthonormal(): pl.pallas_call(orthonormal_kernel, out_shape=jax.ShapeDtypeStruct(p_rows....]
    dot_general x1, matrix products: 7.69 us -> 5.91 us  [shards(): lax.dot_general(left_low, right_low, (((1,), (1,)), ((), ())), preferred_...]
    unnamed x4 -> x8, local copies, waits for them, and re-layouts: 0.01 us -> 1.67 us
where the time goes in v5:
time: 82.2 us; the launch traced here: 82 us
  Pallas kernels  72.2 us (88%)
  matrix products  5.91 us (7%)
  local copies, waits for them, and re-layouts  1.67 us (2%)
  other arithmetic  1.52 us (2%)
    pallas_call x1, Pallas kernels, right_mean(): pl.pallas_call(functools.partial(right_kernel, replicas, inner, chunks, r...  39.2 us
    pallas_call x1, Pallas kernels, left_sum(): pl.pallas_call(functools.partial(left_kernel, replicas, tensors, chunks,...  27.7 us
    dot_general x1, matrix products, shards(): lax.dot_general(left_low, right_low, (((1,), (1,)), ((), ())), preferred_...  5.91 us
    pallas_call x1, Pallas kernels, orthonormal(): pl.pallas_call(orthonormal_kernel, out_shape=jax.ShapeDtypeStruct(p_rows....  5.34 us
    unnamed x8, local copies, waits for them, and re-layouts  1.67 us

profile of v5, /device:TPU:0, one launch (start us, length us, event | category | flops | bytes accessed | tf_op | source)
XLA Modules:
  0.0 82.0 jit_solution(15145475818247383155)
XLA Ops:
  0.6 27.7 %shard_map.59 = (bf16[768,4096]{1,0:T(8,128)(2,1)}, f32[3,2,16,8,128]{4,3,2,1,0:T(8,128)}) custom-call(bf16[512,4096]{1,0:T(8,128)(2,1)} %act_hbm.1, bf16[512,768]{1,0:T(8,128)(2,1)} %cot_hbm.1, bf16[1,768,4096]{2,1,0:T(8,128)(2,1)} %err_hbm.1, bf16[4096,128]{1,0:T(8,128)(2,1)} %right_hbm.1), custom_call_target="tpu_custom_call" | custom-call | tf_op jit(solution)/shard_map/pallas_call | solution.py:156
  28.4 0.0 copy-start.1
  28.4 1.0 %copy-done.1 = f32[3,2,16,8,128]{4,3,2,1,0:T(8,128)S(1)} copy-done((f32[3,2,16,8,128]{4,3,2,1,0:T(8,128)S(1)}, f32[3,2,16,8,128]{4,3,2,1,0:T(8,128)}, u32[]{:S(2)}) %copy-start.1) | copy-done | bytes 393240
  29.4 0.0 copy-start.2
  29.4 5.3 %shard_map.60.left_ref = bf16[768,128]{1,0:T(8,128)(2,1)S(1)} custom-call(f32[768,128]{1,0:T(8,128)S(1)} %bitcast.7), custom_call_target="tpu_custom_call" | custom-call | tf_op jit(solution)/shard_map/pallas_call | solution.py:359
  34.7 0.0 copy-start
  34.7 0.7 copy-done
  35.4 39.2 %shard_map.61 = bf16[2,8,4,64,128]{4,3,2,1,0:T(8,128)(2,1)} custom-call(bf16[768,4096]{1,0:T(8,128)(2,1)} %get-tuple-element.4.comp_hbm, bf16[768,128]{1,0:T(8,128)(2,1)} %copy-done), custom_call_target="tpu_custom_call" | custom-call | tf_op jit(solution)/shard_map/pallas_call | solution.py:292
  74.6 0.0 copy-done.2
  74.6 0.0 copy-start.3
  74.6 5.9 %fusion = bf16[1,768,4096]{2,1,0:T(8,128)(2,1)} fusion(bf16[768,128]{1,0:T(8,128)(2,1)} %copy-done, bf16[4096,128]{1,0:T(8,128)(2,1)} %bitcast.8, bf16[768,4096]{1,0:T(8,128)(2,1)S(1)} %copy-done.2), kind=kOutput, calls=%fused_computation.1 | convolution fusion | flops 814743552 | bytes 13828096 | tf_op jit(solution)/shard_map/dot_general | solution.py:374
  80.5 0.0 copy-done.3
  80.5 1.5 %bitcast_convert_fusion = f32[4096,128]{1,0:T(8,128)} fusion(bf16[2,8,4,64,128]{4,3,2,1,0:T(8,128)(2,1)S(1)} %copy-done.3), kind=kLoop, calls=%fused_computation.2 | loop fusion | flops 524288 | bytes 3145728 | tf_op jit(solution)/shard_map/convert_element_type | solution.py:373
Async XLA Ops:
  28.4 1.0 %copy-start.1 = (f32[3,2,16,8,128]{4,3,2,1,0:T(8,128)S(1)}, f32[3,2,16,8,128]{4,3,2,1,0:T(8,128)}, u32[]{:S(2)}) copy-start(f32[3,2,16,8,128]{4,3,2,1,0:T(8,128)} %get-tuple-element.5) | copy-start | bytes 1179652
  29.4 45.2 %copy-start.2 = (bf16[768,4096]{1,0:T(8,128)(2,1)S(1)}, bf16[768,4096]{1,0:T(8,128)(2,1)}, u32[]{:S(2)}) copy-start(bf16[768,4096]{1,0:T(8,128)(2,1)} %get-tuple-element.4.comp_hbm) | copy-start | bytes 18874372
  34.7 0.7 copy-start
  74.6 5.9 %copy-start.3 = (bf16[2,8,4,64,128]{4,3,2,1,0:T(8,128)(2,1)S(1)}, bf16[2,8,4,64,128]{4,3,2,1,0:T(8,128)(2,1)}, u32[]{:S(2)}) copy-start(bf16[2,8,4,64,128]{4,3,2,1,0:T(8,128)(2,1)} %shard_map.61) | copy-start | bytes 3145732
